TPU v7x, 256 devices: a whole 4x4x8 slice. The times are simulated.
256 devices in a mesh: row: 32 (over y, z), col: 8 (over x, core).
Axes of the slice: x: 4, y: 4, z: 8, core: 2. Of those that a mesh axis runs over, the one named last changes fastest.
Arguments:
- trail_adjoint: float32 [24576, 24576], P('row', 'col'), may hold values from -3 to 3
- panel: float32 [24576, 256], P(('row', 'col')), may hold values from -0.0390625 to 0.0390625
- panel_adjoint: float32 [24576, 256], P(('row', 'col')), may hold values from -6 to 6
- diag_factor: float32 [256, 256], replicated, as said below
- diag_inverse: float32 [256, 256], replicated, as said below
- diag_adjoint: float32 [256, 256], replicated, may hold values from -6 to 6
Outputs:
- panel_grad: float32 [24576, 256], P(('row', 'col'))
- diag_grad: float32 [256, 256], replicated
Inputs may be any that keep to these rules, and one draw needn't show every extreme that they name: diag_factor is lower triangular with a diagonal between 1 and 2, and diag_inverse is its inverse. diag_factor is lower triangular with a diagonal between 1 and 2.
All inputs are finite; a program needn't handle non-finite values.
Results may differ from a plain program's by a relative error of at most 0.000057.
Values sent between devices are 32-bit elements; how exact they have to be, the bound alone decides.
A program may use at most 128 MiB of HBM per device.

v0:
```python
import jax
import jax.numpy as jnp
from jax import lax
from jax.sharding import PartitionSpec as P


def lower_half(matrix):
    return jnp.tril(matrix) - 0.5 * jnp.diag(jnp.diag(matrix))


def on_device(trail_adjoint, panel, panel_adjoint, diag_factor, diag_inverse, diag_adjoint):
    highest = lax.Precision.HIGHEST
    col_place = lax.axis_index("col")
    trail_width = trail_adjoint.shape[1]
    row_block = lax.all_gather(panel, "col", axis=0, tiled=True)
    full_panel = lax.all_gather(row_block, "row", axis=0, tiled=True)
    column_panel = lax.dynamic_slice_in_dim(full_panel, col_place * trail_width, trail_width, 0)
    image = lax.psum_scatter(
        jnp.dot(trail_adjoint, column_panel, precision=highest, preferred_element_type=jnp.float32),
        "col",
        scatter_dimension=0,
        tiled=True,
    )
    updated = panel_adjoint - 2.0 * image
    panel_grad = jnp.dot(
        updated, diag_inverse, precision=highest, preferred_element_type=jnp.float32
    )
    local_gram = jnp.dot(panel_grad.T, panel, precision=highest, preferred_element_type=jnp.float32)
    gram = lax.psum(local_gram, ("row", "col"))
    corner = diag_adjoint - gram
    inner = lower_half(
        jnp.dot(diag_factor.T, corner, precision=highest, preferred_element_type=jnp.float32)
    )
    left_part = jnp.dot(
        diag_inverse.T, inner, precision=highest, preferred_element_type=jnp.float32
    )
    diag_grad = lower_half(
        jnp.dot(left_part, diag_inverse, precision=highest, preferred_element_type=jnp.float32)
    )
    return (panel_grad, diag_grad)


def solution(mesh):
    in_specs = (P("row", "col"), P(("row", "col"), None), P(("row", "col"), None), P(), P(), P())
    out_specs = (P(("row", "col"), None), P())
    return jax.shard_map(
        on_device, mesh=mesh, in_specs=in_specs, out_specs=out_specs, check_vma=False
    )
```

profile of v0, /device:TPU:1, one launch (start us, length us, event | category | flops | bytes accessed | tf_op | source)
XLA Modules:
  0.0 521.9 jit_solution(10304371956958443014)
XLA Ops:
  7.2 0.0 copy-start
  7.2 0.0 copy-start.1
  7.2 0.0 copy-start.5
  7.2 0.0 all-gather.2.cloned.1.call-start
  7.3 17.9 %all_gather.6 = f32[768,256]{1,0:T(8,128)} all-gather(f32[96,256]{1,0:T(8,128)} %param.7), channel_id=1, replica_groups=mesh['row'=32,'col'=8] {'col'}, dimensions={0}, use_global_device_ids=true | all-gather | bytes 884736 | tf_op jit(solution)/shard_map/all_gather | solution.py:15
  25.2 0.0 all-gather.2.cloned.1.call-update
  25.2 0.0 reduce-scatter.2.cloned.1.call-start
  25.2 184.0 %all-gather.2.cloned.1.call-done = f32[24576,256]{1,0:T(8,128)} async-done(((f32[768,256]{1,0:T(8,128)}), f32[24576,256]{1,0:T(8,128)}) %all-gather.2.cloned.1.call-update) | async-done | bytes 25165840 | tf_op jit(solution)/shard_map/all_gather | solution.py:16
  209.2 11.5 %fusion.2 = f32[768,256]{1,0:T(8,128)} fusion(f32[768,3072]{1,0:T(8,128)} %param.6, f32[24576,256]{1,0:T(8,128)} %all-gather.2.cloned.1.call-done, s32[]{:T(128)S(6)} %select_n.26), kind=kOutput, calls=%fused_computation.4 | convolution fusion | flops 7247757312 | bytes 13369348 | tf_op jit(solution)/shard_map/dot_general | solution.py:19
  220.7 0.0 reduce-scatter.2.cloned.1.call-update
  220.7 0.0 all-reduce.2.cloned.1.call-start
  220.8 29.1 %reduce-scatter.2.cloned.1.call-done = f32[96,256]{1,0:T(8,128)} async-done(((f32[768,256]{1,0:T(8,128)}), f32[96,256]{1,0:T(8,128)}) %reduce-scatter.2.cloned.1.call-update) | async-done | bytes 98320 | tf_op jit(solution)/shard_map/reduce_scatter | solution.py:18
  249.9 1.2 fusion.14
  251.0 0.0 copy-start.2
  251.0 1.1 fusion.22
  252.2 0.0 all-reduce.2.cloned.1.call-update
  252.2 254.8 %all-reduce.2.cloned.1.call-done = f32[256,256]{1,0:T(8,128)} async-done(((f32[256,256]{1,0:T(8,128)}), f32[256,256]{1,0:T(8,128)}) %all-reduce.2.cloned.1.call-update) | async-done | bytes 262160 | tf_op jit(solution)/shard_map/psum | solution.py:29
  507.0 1.5 convolution_bitcast_fusion
  508.6 2.4 gather_fusion
  511.0 0.4 fusion.5
  511.4 0.6 fusion.23
  512.0 0.1 copy.10
  512.1 2.3 gather_fusion.1
  514.5 0.8 copy.11
  (10 shorter events, 0.1 us)
Async XLA Ops:
  7.2 242.7 %copy-start = (f32[256,256]{1,0:T(8,128)S(1)}, f32[256,256]{1,0:T(8,128)}, u32[]{:S(2)}) copy-start(f32[256,256]{1,0:T(8,128)} %param.10) | copy-start | bytes 786436
  7.2 243.8 %copy-start.1 = (f32[96,256]{1,0:T(8,128)S(1)}, f32[96,256]{1,0:T(8,128)}, u32[]{:S(2)}) copy-start(f32[96,256]{1,0:T(8,128)} %param.7) | copy-start | bytes 294916
  7.2 242.7 %copy-start.5 = (f32[96,256]{1,0:T(8,128)S(1)}, f32[96,256]{1,0:T(8,128)}, u32[]{:S(2)}) copy-start(f32[96,256]{1,0:T(8,128)} %param.8) | copy-start | bytes 294916
  7.2 499.8 %copy-start.3 = (f32[256,256]{1,0:T(8,128)S(1)}, f32[256,256]{1,0:T(8,128)}, u32[]{:S(2)}) copy-start(f32[256,256]{1,0:T(8,128)} %param.9) | copy-start | bytes 786436
  7.2 499.8 %copy-start.4 = (f32[256,256]{1,0:T(8,128)S(1)}, f32[256,256]{1,0:T(8,128)}, u32[]{:S(2)}) copy-start(f32[256,256]{1,0:T(8,128)} %param.11) | copy-start | bytes 786436
  7.2 202.0 %all-gather.2.cloned.1.call-start = ((), (), s32[]{:S(2)}) async-start(), calls=%async_computation.1 | async-start | bytes 25952256 | tf_op jit(solution)/shard_map/all_gather | solution.py:16
  25.2 224.7 %reduce-scatter.2.cloned.1.call-start = ((), (), s32[]{:S(2)}) async-start(), calls=%async_computation.2 | async-start | bytes 884736 | tf_op jit(solution)/shard_map/reduce_scatter | solution.py:18
  220.7 286.3 %all-reduce.2.cloned.1.call-start = ((), (), s32[]{:S(2)}) async-start(), calls=%async_computation.3 | async-start | bytes 524288 | tf_op jit(solution)/shard_map/psum | solution.py:29
  251.0 264.3 %copy-start.2 = (f32[96,256]{1,0:T(8,128)}, f32[96,256]{1,0:T(8,128)S(1)}, u32[]{:S(2)}) copy-start(f32[96,256]{1,0:T(8,128)S(1)} %fusion.14) | copy-start | bytes 294916
Sparse Core Ops, SparseCore 0:
  25.3 183.8 all-gather.1
  220.9 28.9 reduce-scatter.1
  256.8 250.2 all-reduce.1
where the time goes:
time: 523 us; the launch traced here: 522 us
  waiting for transfers between devices  468 us (89%)
  blocking collectives  17.9 us (3%)
  matrix products  16.3 us (3%)
  between operations  13.9 us (3%)
  local copies, waits for them, and re-layouts  5.71 us (1%)
    psum x1, waiting for transfers between devices, on_device(): gram = lax.psum(local_gram, ('row', 'col'))  255 us
    all_gather x1, waiting for transfers between devices, on_device(): full_panel = lax.all_gather(row_block, 'row', axis=0, tiled=True)  184 us
    reduce_scatter x1, waiting for transfers between devices, on_device(): lax.psum_scatter(jnp.dot(trail_adjoint, column_panel, precision=highest,...  29.1 us
    all_gather x1, blocking collectives, on_device(): row_block = lax.all_gather(panel, 'col', axis=0, tiled=True)  17.9 us
    dot_general x1, matrix products, on_device(): jnp.dot(trail_adjoint, column_panel, precision=highest, preferred_element...  11.5 us
  transfers between devices with their start and end apart: 3, of which 3 were waited for; matrix products, arithmetic and copies ran while one was open for 0% of the time, Pallas kernels for 0%

commit v1 on v0

v1 whole, which is shorter than its diff:
```python
import jax
import jax.numpy as jnp
from jax import lax
from jax.experimental import pallas as pl
from jax.experimental.pallas import tpu as pltpu
from jax.sharding import PartitionSpec as P

MESH = pl.DeviceIdType.MESH
F32 = jnp.float32
BF16 = jnp.bfloat16
HIGHEST = lax.Precision.HIGHEST

NX, NY, NZ = 4, 4, 8
ROWS = 96
WIDE = 256
CHUNK = 768
FIRST = 48
SECOND = ROWS - FIRST
CUT = 24


def dot(a, b):
    return jnp.dot(a, b, precision=HIGHEST, preferred_element_type=F32)


def lower_half(matrix):
    i = lax.broadcasted_iota(jnp.int32, matrix.shape, 0)
    j = lax.broadcasted_iota(jnp.int32, matrix.shape, 1)
    return jnp.where(i > j, matrix, jnp.where(i == j, 0.5 * matrix, 0.0))


def kernel(
    trail, panel, panel_adjoint, diag_factor, diag_inverse, diag_adjoint,
    panel_grad, diag_grad,
    raw, high, low, gathered, ring, p_high, p_low, image, parts,
    gram_local, gram_parts, tiles, tile_parts, row_tiles, all_tiles, gram,
    trail_sem,
    s1u_send, s1u_recv, s1z_send, s1z_recv,
    s2z_send, s2z_recv, s2u_send, s2u_recv,
    rs_send, rs_recv, ga_send, ga_recv, gb_send, gb_recv,
    gc_send, gc_recv, gd_send, gd_recv,
):
    r = lax.axis_index("row")
    q = lax.axis_index("col")
    y, z = r // NZ, r % NZ
    x, c = q // 2, q % 2
    half = z // 4

    loads = [
        pltpu.make_async_copy(
            trail.at[:, pl.ds(j * CHUNK, CHUNK)], raw.at[j], trail_sem.at[j]
        )
        for j in range(4)
    ]
    for load in loads:
        load.start()

    def col_peer(dx, dc):
        return ((x + dx) % NX) * 2 + (c + dc) % 2

    barrier = pltpu.get_barrier_semaphore()

    def greet(row, col):
        pl.semaphore_signal(barrier, inc=1, device_id=(row, col), device_id_type=MESH)

    for dx in range(4):
        for dc in range(2):
            if (dx, dc) == (0, 0):
                @pl.when(x != y)
                def _():
                    greet(x * NZ + z, q)
            else:
                greet(x * NZ + z, col_peer(dx, dc))
    for dy in range(4):
        for dz in range(8):
            if (dy, dz) != (0, 0):
                greet(((y + dy) % NY) * NZ + (z + dz) % NZ, q)
    for dx in range(4):
        for dc in range(2):
            if (dx, dc) != (0, 0):
                greet(r, col_peer(dx, dc))

    ring[z] = panel[FIRST:, :]
    image[...] = jnp.zeros_like(image)

    @pl.when(x == y)
    def _():
        pl.semaphore_wait(barrier, 7 + 31 + 7)

    @pl.when(x != y)
    def _():
        pl.semaphore_wait(barrier, 8 + 31 + 7)

    sent = []

    def remote(src, dst, send, recv, row, col):
        return pltpu.make_async_remote_copy(
            src_ref=src, dst_ref=dst, send_sem=send, recv_sem=recv,
            device_id=(row, col), device_id_type=MESH,
        )

    def go(copy):
        copy.start()
        sent.append((None, copy))

    def spread(src, slot, rows, core, send, recv):
        dst = gathered.at[slot, q, rows]
        for dy in (2, 1, 3, 0):
            copy = remote(src, dst, send.at[dy], recv, ((y + dy) % NY) * NZ + z, 2 * y + core)
            if dy:
                go(copy)
            else:
                own = (x == y) & (core == c)

                @pl.when(own)
                def _():
                    pltpu.make_async_copy(src, dst, recv).start()

                @pl.when(jnp.logical_not(own))
                def _():
                    copy.start()

                sent.append((jnp.logical_not(own), copy))

    top, bottom = pl.ds(0, FIRST), pl.ds(FIRST, SECOND)
    up, down = y * NZ + (z + 1) % NZ, y * NZ + (z + 7) % NZ
    towards = (up, down)

    def origin(way, s):
        return (z - s + 8) % NZ if way == 0 else (z + s) % NZ

    def ring_part(o, way, s):
        if s < 4:
            return ring.at[o]
        return ring.at[o, pl.ds(0, CUT)] if way == 0 else ring.at[o, pl.ds(CUT, SECOND - CUT)]

    def bundle_part(o, way, s):
        if s < 4:
            return gathered.at[o % 4, :, top]
        return gathered.at[o % 4, pl.ds(4 * way, 4), top]

    def s2z(way, s):
        ref = ring_part(origin(way, s - 1), way, s)
        return remote(ref, ref, s2z_send.at[way, s - 1], s2z_recv.at[way, s - 1], towards[way], q)

    def s2z_wait(way, s):
        ref = ring_part(origin(way, s), way, s)
        remote(ref, ref, s2z_send.at[way, s - 1], s2z_recv.at[way, s - 1], towards[way], q).wait_recv()

    def s2u(way, s):
        o = origin(way, s)
        spread(ring.at[o], o % 4, bottom, o // 4, s2u_send.at[way, s], s2u_recv.at[o % 4])

    def s1z_start(s):
        for way in range(2):
            o = origin(way, s - 1)
            ref = bundle_part(o, way, s)
            copy = remote(ref, ref, s1z_send.at[way, s - 1], s1z_recv.at[way, s - 1], towards[way], q)
            mine = o // 4 == c

            @pl.when(mine)
            def _():
                copy.start()

            sent.append((mine, copy))

    def s1z_wait(s):
        for way in range(2):
            o = origin(way, s)

            @pl.when(o // 4 == c)
            def _():
                ref = bundle_part(o, way, s)
                remote(
                    ref, ref, s1z_send.at[way, s - 1], s1z_recv.at[way, s - 1], towards[way], q
                ).wait_recv()

    def split_trail(j):
        loads[j].wait()

        @pl.loop(0, CHUNK, step=32)
        def _(i):
            rows = pl.ds(pl.multiple_of(i, 32), 32)
            value = raw[j, rows, :]
            head = value.astype(BF16)
            high[j, rows, :] = head
            low[j, rows, :] = (value - head.astype(F32)).astype(BF16)

    def multiply(o):
        @pl.when(o // 4 == c)
        def _():
            j = o % 4
            pltpu.make_async_copy(
                gathered.at[j, :, bottom], gathered.at[j, :, bottom], s2u_recv.at[j]
            ).wait()
            block = gathered[j].reshape(CHUNK, WIDE)
            head = block.astype(BF16)
            p_high[...] = head
            p_low[...] = (block - head.astype(F32)).astype(BF16)

            @pl.loop(0, CHUNK, step=256)
            def _(i):
                rows = pl.ds(pl.multiple_of(i, 256), 256)
                a, b = high[j, rows, :], low[j, rows, :]
                image[rows, :] += (
                    jnp.dot(a, p_high[...], preferred_element_type=F32)
                    + jnp.dot(a, p_low[...], preferred_element_type=F32)
                    + jnp.dot(b, p_high[...], preferred_element_type=F32)
                )

    spread(panel.at[top], z % 4, top, half, s1u_send, s1u_recv)
    go(s2z(0, 1))
    go(s2z(1, 1))
    s2u(0, 0)
    split_trail(0)

    @pl.when(half == c)
    def _():
        ref = gathered.at[z % 4, :, top]
        pltpu.make_async_copy(ref, ref, s1u_recv).wait()

    s1z_start(1)
    for s in (1, 2, 3):
        for way in range(2):
            s2z_wait(way, s)
            go(s2z(way, s + 1))
            s2u(way, s)
        if s == 1:
            split_trail(1)
        if s == 2:
            s1z_wait(1)
            s1z_start(2)
            split_trail(2)
    for way in range(2):
        s2z_wait(way, 4)
    s2u(0, 4)
    split_trail(3)
    multiply(z)
    s1z_wait(2)
    s1z_start(3)
    multiply(origin(0, 1))
    multiply(origin(1, 1))
    s1z_wait(3)
    s1z_start(4)
    for s in (2, 3):
        multiply(origin(0, s))
        multiply(origin(1, s))
    s1z_wait(4)
    multiply(origin(0, 4))

    peers = [(dx, dc) for dx in (2, 1, 3, 0) for dc in (0, 1) if (dx, dc) != (0, 0)]
    for n, (dx, dc) in enumerate(peers):
        to = col_peer(dx, dc)
        go(remote(
            image.at[pl.ds(pl.multiple_of(to * ROWS, ROWS), ROWS)], parts.at[n],
            rs_send.at[n], rs_recv, r, to,
        ))
    pltpu.make_async_copy(parts, parts, rs_recv).wait()
    total = image[pl.ds(pl.multiple_of(q * ROWS, ROWS), ROWS), :]
    for n in range(7):
        total = total + parts[n]
    updated = panel_adjoint[...] - 2.0 * total
    grad = dot(updated, diag_inverse[...])
    panel_grad[...] = grad
    gram_local[...] = dot(grad.T, panel[...])

    for n, (dx, dc) in enumerate(peers):
        to = col_peer(dx, dc)
        go(remote(
            gram_local.at[pl.ds(pl.multiple_of(to * 32, 32), 32)], gram_parts.at[n],
            ga_send.at[n], ga_recv, r, to,
        ))
    pltpu.make_async_copy(gram_parts, gram_parts, ga_recv).wait()
    slab = gram_local[pl.ds(pl.multiple_of(q * 32, 32), 32), :]
    for n in range(7):
        slab = slab + gram_parts[n]
    for t in range(8):
        tiles[t] = slab[8 * (t // 2) : 8 * (t // 2) + 8, 128 * (t % 2) : 128 * (t % 2) + 128]
    n = 0
    for dz in (4, 3, 5, 2, 6, 1, 7, 0):
        for dy in (2, 1, 3, 0):
            if (dy, dz) != (0, 0):
                to_z = (z + dz) % NZ
                go(remote(
                    tiles.at[to_z], tile_parts.at[r], gb_send.at[n], gb_recv,
                    ((y + dy) % NY) * NZ + to_z, q,
                ))
                n += 1
    tile_parts[r] = tiles[z]
    pltpu.make_async_copy(
        tile_parts.at[pl.ds(0, 31)], tile_parts.at[pl.ds(0, 31)], gb_recv
    ).wait()
    row_tiles[z] = jnp.sum(tile_parts[...], axis=0)
    for n, dz in enumerate((4, 3, 5, 2, 6, 1, 7)):
        go(remote(
            row_tiles.at[z], row_tiles.at[z], gc_send.at[n], gc_recv, y * NZ + (z + dz) % NZ, q,
        ))
    pltpu.make_async_copy(row_tiles.at[pl.ds(0, 7)], row_tiles.at[pl.ds(0, 7)], gc_recv).wait()
    for n, (dx, dc) in enumerate(peers):
        go(remote(row_tiles, all_tiles.at[q], gd_send.at[n], gd_recv, r, col_peer(dx, dc)))
    all_tiles[q] = row_tiles[...]
    pltpu.make_async_copy(
        all_tiles.at[pl.ds(0, 7)], all_tiles.at[pl.ds(0, 7)], gd_recv
    ).wait()
    for k in range(8):
        for t in range(8):
            i, j = 32 * k + 8 * (t // 2), 128 * (t % 2)
            gram[i : i + 8, j : j + 128] = all_tiles[k, t]

    corner = diag_adjoint[...] - gram[...]
    inner = lower_half(dot(diag_factor[...].T, corner))
    left = dot(diag_inverse[...].T, inner)
    diag_grad[...] = lower_half(dot(left, diag_inverse[...]))

    for condition, copy in sent:
        if condition is None:
            copy.wait_send()
        else:
            pl.when(condition)(copy.wait_send)


def on_device(trail_adjoint, panel, panel_adjoint, diag_factor, diag_inverse, diag_adjoint):
    vmem = pl.BlockSpec(memory_space=pltpu.VMEM)
    dma = pltpu.SemaphoreType.DMA
    return pl.pallas_call(
        kernel,
        out_shape=(
            jax.ShapeDtypeStruct((ROWS, WIDE), F32),
            jax.ShapeDtypeStruct((WIDE, WIDE), F32),
        ),
        in_specs=[pl.BlockSpec(memory_space=pl.ANY)] + [vmem] * 5,
        out_specs=(vmem, vmem),
        scratch_shapes=[
            pltpu.VMEM((4, CHUNK, CHUNK), F32),
            pltpu.VMEM((4, CHUNK, CHUNK), BF16),
            pltpu.VMEM((4, CHUNK, CHUNK), BF16),
            pltpu.VMEM((4, 8, ROWS, WIDE), F32),
            pltpu.VMEM((8, SECOND, WIDE), F32),
            pltpu.VMEM((CHUNK, WIDE), BF16),
            pltpu.VMEM((CHUNK, WIDE), BF16),
            pltpu.VMEM((CHUNK, WIDE), F32),
            pltpu.VMEM((7, ROWS, WIDE), F32),
            pltpu.VMEM((WIDE, WIDE), F32),
            pltpu.VMEM((7, 32, WIDE), F32),
            pltpu.VMEM((8, 8, 128), F32),
            pltpu.VMEM((32, 8, 128), F32),
            pltpu.VMEM((8, 8, 128), F32),
            pltpu.VMEM((8, 8, 8, 128), F32),
            pltpu.VMEM((WIDE, WIDE), F32),
            dma((4,)),
            dma((4,)), dma, dma((2, 4)), dma((2, 4)),
            dma((2, 4)), dma((2, 4)), dma((2, 5, 4)), dma((4,)),
            dma((7,)), dma, dma((7,)), dma, dma((31,)), dma,
            dma((7,)), dma, dma((7,)), dma,
        ],
        compiler_params=pltpu.CompilerParams(
            collective_id=0, has_side_effects=True, vmem_limit_bytes=56 * 1024 * 1024
        ),
    )(trail_adjoint, panel, panel_adjoint, diag_factor, diag_inverse, diag_adjoint)


def solution(mesh):
    in_specs = (P("row", "col"), P(("row", "col"), None), P(("row", "col"), None), P(), P(), P())
    out_specs = (P(("row", "col"), None), P())
    return jax.shard_map(
        on_device, mesh=mesh, in_specs=in_specs, out_specs=out_specs, check_vma=False
    )
```

time: 523 us -> 129 us (0.25)
  waiting for transfers between devices: 468 us -> 0 us
  Pallas kernels: 0 us -> 125 us
  blocking collectives: 17.9 us -> 0 us
  matrix products: 16.3 us -> 0 us
  between operations: 13.9 us -> 0.64 us
    psum x1 -> x0, waiting for transfers between devices: 255 us -> none  [on_device(): gram = lax.psum(local_gram, ('row', 'col'))]
    all_gather x1 -> x0, waiting for transfers between devices: 184 us -> none  [on_device(): full_panel = lax.all_gather(row_block, 'row', axis=0, tiled=True)]
    pallas_call x0 -> x1, Pallas kernels: none -> 125 us  [on_device(): pl.pallas_call(kernel, out_shape=(jax.ShapeDtypeStruct((ROWS, WIDE), F32)...]
    reduce_scatter x1 -> x0, waiting for transfers between devices: 29.1 us -> none  [on_device(): lax.psum_scatter(jnp.dot(trail_adjoint, column_panel, precision=highest,...]
    all_gather x1 -> x0, blocking collectives: 17.9 us -> none  [on_device(): row_block = lax.all_gather(panel, 'col', axis=0, tiled=True)]
    dot_general x6 -> x0, matrix products: 16.3 us -> none  [the longest x1 11.5 us: on_device(): jnp.dot(trail_adjoint, column_panel, precision=highest, preferred_element...]
  transfers between devices with their start and end apart: 3 -> 0, of which waited for: 3 -> 0; matrix products, arithmetic and copies ran while one was open for 0% -> 0% of each run, Pallas kernels for 0% -> 0%
where the time goes in v1:
time: 129 us
  Pallas kernels  125 us (97%)
  local copies, waits for them, and re-layouts  3.21 us (2%)
    pallas_call x1, Pallas kernels, on_device(): pl.pallas_call(kernel, out_shape=(jax.ShapeDtypeStruct((ROWS, WIDE), F32)...  125 us
    unnamed x2, local copies, waits for them, and re-layouts  3.21 us

profile of v1, /device:TPU:1, one launch (start us, length us, event | category | flops | bytes accessed | tf_op | source)
XLA Modules:
  0.0 128.8 jit_solution(12114415015668806152)
XLA Ops:
  0.6 125.0 %shard_map.77 = (f32[96,256]{1,0:T(8,128)}, f32[256,256]{1,0:T(8,128)}) custom-call(f32[768,3072]{1,0:T(8,128)} %trail.1, f32[96,256]{1,0:T(8,128)} %panel.1, f32[96,256]{1,0:T(8,128)} %panel_adjoint.1, f32[256,256]{1,0:T(8,128)} %diag_factor.1, f32[256,256]{1,0:T(8,128)} %diag_inverse.1, f32[256,256]{1,0:T(8,128)} %diag_adjoint.1), custom_call_target="tpu_custom_call" | custom-call | tf_op jit(solution)/shard_map/pallas_call | solution.py:325
  125.6 1.5 %copy.10 = f32[96,256]{1,0:T(8,128)} copy(f32[96,256]{1,0:T(8,128)} %get-tuple-element.4) | data formatting | bytes 196608
  127.1 1.7 %copy.11 = f32[256,256]{1,0:T(8,128)} copy(f32[256,256]{1,0:T(8,128)} %get-tuple-element.5) | data formatting | bytes 524288

commit v2 on v0

v2 whole, which is shorter than its diff:
```python
import jax
import jax.numpy as jnp
from jax import lax
from jax.experimental import pallas as pl
from jax.experimental.pallas import tpu as pltpu
from jax.sharding import PartitionSpec as P

MESH = pl.DeviceIdType.MESH
F32 = jnp.float32
BF16 = jnp.bfloat16
HIGHEST = lax.Precision.HIGHEST

NX, NY, NZ = 4, 4, 8
ROWS = 96
WIDE = 256
CHUNK = 768
FIRST = 40
SECOND = ROWS - FIRST


def dot(a, b):
    return jnp.dot(a, b, precision=HIGHEST, preferred_element_type=F32)


def lower_half(matrix):
    i = lax.broadcasted_iota(jnp.int32, matrix.shape, 0)
    j = lax.broadcasted_iota(jnp.int32, matrix.shape, 1)
    return jnp.where(i > j, matrix, jnp.where(i == j, 0.5 * matrix, 0.0))


def kernel(
    trail, panel, panel_adjoint, diag_factor, diag_inverse, diag_adjoint,
    panel_grad, diag_grad,
    raw, high, low, gathered, stage, p_high, p_low, image,
    row_panel, turned_high, turned_low, early, chain, base, inverse_t,
    gram_local, gram_parts, slab, slab_parts, gram,
    core_parts, x_source, x_parts,
    trail_sem,
    s1y_send, s1y_recv, s1x_send, s1u_recv, s1z_send, s1z_recv,
    s2r_send, s2r_recv, s2z_send, s2z_recv, s2y_send, s2y_recv,
    rp_send, rp_recv, rc_send, rc_recv, rx_send, rx_recv,
    ga_send, ga_recv, gb_send, gb_recv, gc_send, gc_recv,
):
    r = lax.axis_index("row")
    q = lax.axis_index("col")
    y, z = r // NZ, r % NZ
    x, c = q // 2, q % 2
    half = z // 4

    loads = [
        pltpu.make_async_copy(
            trail.at[:, pl.ds(j * CHUNK, CHUNK)], raw.at[j], trail_sem.at[j]
        )
        for j in range(4)
    ]
    for load in loads:
        load.start()

    def col_peer(dx, dc):
        return ((x + dx) % NX) * 2 + (c + dc) % 2

    plane = [
        (dy, dx, dc)
        for dy in (2, 1, 3, 0)
        for dx in (2, 1, 3, 0)
        for dc in (0, 1)
        if (dy, dx, dc) != (0, 0, 0)
    ]
    row_peers = [(dx, dc) for dy, dx, dc in plane if dy == 0]
    depth = (4, 3, 5, 2, 6, 1, 7)

    def plane_peer(dy, dx, dc):
        return ((y + dy) % NY) * NZ + z, col_peer(dx, dc)

    barrier = pltpu.get_barrier_semaphore()

    def greet(row, col):
        pl.semaphore_signal(barrier, inc=1, device_id=(row, col), device_id_type=MESH)

    for peer in plane:
        greet(*plane_peer(*peer))
    for dz in depth:
        greet(y * NZ + (z + dz) % NZ, q)

    sent = []

    def remote(src, dst, send, recv, row, col):
        return pltpu.make_async_remote_copy(
            src_ref=src, dst_ref=dst, send_sem=send, recv_sem=recv,
            device_id=(row, col), device_id_type=MESH,
        )

    def go(copy):
        copy.start()
        sent.append((None, copy))

    def landed(ref, recv):
        pltpu.make_async_copy(ref, ref, recv).wait()

    def one_or_local(copy, own, src, dst, recv):
        @pl.when(own)
        def _():
            pltpu.make_async_copy(src, dst, recv).start()

        @pl.when(jnp.logical_not(own))
        def _():
            copy.start()

        sent.append((jnp.logical_not(own), copy))

    top, bottom = pl.ds(0, FIRST), pl.ds(FIRST, SECOND)
    towards = (y * NZ + (z + 1) % NZ, y * NZ + (z + 7) % NZ)

    def origin(way, s):
        return (z - s + 8) % NZ if way == 0 else (z + s) % NZ

    def top_copy(o, way, s, part):
        ref = gathered.at[o % 4, pl.ds(2 * part, 2), top]
        return remote(
            ref, ref, s1z_send.at[way, s - 1, part], s1z_recv.at[way, s - 1, part], towards[way], q
        )

    def bottom_copy(o, way, s):
        items = pl.ds(2 * y, 2) if s < 4 else pl.ds(2 * y + way, 1)
        ref = gathered.at[o % 4, items, bottom]
        return remote(ref, ref, s2z_send.at[way, s - 1], s2z_recv.at[way, s - 1], towards[way], q)

    def carried(way, s, part):
        return s < 4 or part // 2 == way

    def top_start(s, part):
        for way in range(2):
            if carried(way, s, part):
                o = origin(way, s - 1)
                copy = top_copy(o, way, s, part)
                pl.when(o // 4 == c)(copy.start)
                sent.append((o // 4 == c, copy))

    def top_wait(s, part):
        for way in range(2):
            if carried(way, s, part):
                o = origin(way, s)
                pl.when(o // 4 == c)(top_copy(o, way, s, part).wait_recv)

    def top_step(s, *parts):
        for part in parts:
            top_wait(s, part)
            top_start(s + 1, part)

    def bottom_start(s):
        for way in range(2):
            o = origin(way, s - 1)
            copy = bottom_copy(o, way, s)
            pl.when(o // 4 == c)(copy.start)
            sent.append((o // 4 == c, copy))

    def bottom_wait(s):
        for way in range(2):
            o = origin(way, s)
            pl.when(o // 4 == c)(bottom_copy(o, way, s).wait_recv)

    def bottom_step(s):
        bottom_wait(s)
        bottom_start(s + 1)
        s2y(0, s)
        s2y(1, s)

    def s1x(a, src, n):
        dst = gathered.at[z % 4, q, top]
        copy = remote(src, dst, s1x_send.at[n], s1u_recv, r, 2 * a + half)
        one_or_local(copy, (x == a) & (half == c), src, dst, s1u_recv)

    def s2y(way, s):
        o = origin(way, s)
        mine = o // 4 == c
        ref = gathered.at[o % 4, pl.ds(2 * y, 2), bottom]
        for n, dy in enumerate((2, 1, 3)):
            copy = remote(
                ref, ref, s2y_send.at[way, s, n], s2y_recv.at[o % 4],
                ((y + dy) % NY) * NZ + z, q,
            )
            pl.when(mine)(copy.start)
            sent.append((mine, copy))

    def split_trail(j):
        loads[j].wait()

        @pl.loop(0, CHUNK, step=32)
        def _(i):
            rows = pl.ds(pl.multiple_of(i, 32), 32)
            value = raw[j, rows, :]
            head = value.astype(BF16)
            high[j, rows, :] = head
            low[j, rows, :] = (value - head.astype(F32)).astype(BF16)

    def multiply(o):
        @pl.when(o // 4 == c)
        def _():
            j = o % 4
            landed(gathered.at[j, pl.ds(0, 6), bottom], s2y_recv.at[j])
            block = gathered[j].reshape(CHUNK, WIDE)
            head = block.astype(BF16)
            p_high[...] = head
            p_low[...] = (block - head.astype(F32)).astype(BF16)

            @pl.loop(0, CHUNK, step=256)
            def _(i):
                rows = pl.ds(pl.multiple_of(i, 256), 256)
                a, b = high[j, rows, :], low[j, rows, :]
                image[rows, :] += (
                    jnp.dot(a, p_high[...], preferred_element_type=F32)
                    + jnp.dot(a, p_low[...], preferred_element_type=F32)
                    + jnp.dot(b, p_high[...], preferred_element_type=F32)
                )

    image[...] = jnp.zeros_like(image)
    row_panel[q] = panel[...]
    inverse_t[...] = diag_inverse[...].T
    factor_t = diag_factor[...].T
    chain[...] = dot(factor_t, inverse_t[...])
    base[...] = dot(factor_t, diag_adjoint[...])
    early[...] = dot(panel[...].T, panel_adjoint[...])
    for j in range(4):
        split_trail(j)
    pl.semaphore_wait(barrier, len(plane) + len(depth))

    for n, dy in enumerate((2, 1, 3)):
        go(remote(
            panel.at[top], stage.at[3 - n], s1y_send.at[n], s1y_recv.at[3 - n],
            ((y + dy) % NY) * NZ + z, q,
        ))
    s2r_dst = gathered.at[z % 4, q, bottom]
    s2r = remote(panel.at[bottom], s2r_dst, s2r_send, s2r_recv, x * NZ + z, 2 * y + half)
    one_or_local(s2r, (x == y) & (half == c), panel.at[bottom], s2r_dst, s2r_recv)
    s1x(y, panel.at[top], 0)
    for n, dy in ((1, 1), (2, 3), (0, 2)):
        landed(stage.at[3 - n], s1y_recv.at[3 - n])
        s1x((y - dy + NY) % NY, stage.at[3 - n], 3 - n)

    @pl.when(half == c)
    def _():
        landed(gathered.at[z % 4, pl.ds(0, 2), bottom], s2r_recv)

    bottom_start(1)
    s2y(0, 0)
    for n, (dx, dc) in enumerate(row_peers):
        go(remote(panel, row_panel.at[q], rp_send.at[n], rp_recv, r, col_peer(dx, dc)))

    @pl.when(half == c)
    def _():
        landed(gathered.at[z % 4, :, top], s1u_recv)

    for part in range(4):
        top_start(1, part)
    bottom_step(1)
    top_step(1, 0, 1)
    bottom_step(2)
    top_step(1, 2, 3)
    multiply(z)
    top_step(2, 0, 1)
    bottom_step(3)
    top_step(2, 2, 3)
    multiply(origin(0, 1))
    multiply(origin(1, 1))
    top_wait(3, 0)
    top_start(4, 0)
    top_wait(3, 1)
    top_start(4, 1)
    top_wait(3, 2)
    top_start(4, 2)
    top_wait(3, 3)
    top_start(4, 3)
    bottom_wait(4)
    s2y(0, 4)
    landed(row_panel.at[pl.ds(0, 7)], rp_recv)
    turned = row_panel[...].reshape(CHUNK, WIDE).T
    turned_head = turned.astype(BF16)
    turned_high[...] = turned_head
    turned_low[...] = (turned - turned_head.astype(F32)).astype(BF16)
    for s in (2, 3):
        multiply(origin(0, s))
        multiply(origin(1, s))
    for part in range(4):
        top_wait(4, part)
    multiply(origin(0, 4))

    for n in range(4):
        block = pl.ds(pl.multiple_of((2 * n + 1 - c) * ROWS, ROWS), ROWS)
        go(remote(image.at[block], core_parts.at[n], rc_send.at[n], rc_recv, r, col_peer(0, 1)))

    value = image[...]
    head = value.astype(BF16)
    tail = (value - head.astype(F32)).astype(BF16)
    gram_local[...] = early[...] - 2.0 * (
        jnp.dot(turned_high[...], head, preferred_element_type=F32)
        + jnp.dot(turned_high[...], tail, preferred_element_type=F32)
        + jnp.dot(turned_low[...], head, preferred_element_type=F32)
    )
    me = 8 * y + q
    for n, peer in enumerate(plane):
        row, col = plane_peer(*peer)
        to = 8 * (row // NZ) + col
        go(remote(
            gram_local.at[pl.ds(pl.multiple_of(to * 8, 8), 8)], gram_parts.at[me],
            ga_send.at[n], ga_recv, row, col,
        ))
    gram_parts[me] = gram_local[pl.ds(pl.multiple_of(me * 8, 8), 8), :]
    landed(core_parts, rc_recv)
    for n in range(4):
        block = pl.ds(pl.multiple_of((2 * n + c) * ROWS, ROWS), ROWS)
        x_source[n] = image[block, :] + core_parts[n]
    landed(gram_parts.at[pl.ds(0, 31)], ga_recv)
    slab[...] = jnp.sum(gram_parts[...], axis=0)
    for n, dz in enumerate(depth):
        go(remote(
            slab, slab_parts.at[z], gb_send.at[n], gb_recv, y * NZ + (z + dz) % NZ, q,
        ))
    slab_parts[z] = slab[...]
    for n, dx in enumerate((2, 1, 3)):
        to = (x + dx) % NX
        go(remote(x_source.at[to], x_parts.at[n], rx_send.at[n], rx_recv, r, 2 * to + c))
    landed(slab_parts.at[pl.ds(0, 7)], gb_recv)
    mine = pl.ds(pl.multiple_of(me * 8, 8), 8)
    gram[mine, :] = jnp.sum(slab_parts[...], axis=0)
    for n, peer in enumerate(plane):
        go(remote(gram.at[mine], gram.at[mine], gc_send.at[n], gc_recv, *plane_peer(*peer)))

    landed(x_parts, rx_recv)
    total = x_source[x] + x_parts[0] + x_parts[1] + x_parts[2]
    panel_grad[...] = dot(panel_adjoint[...] - 2.0 * total, diag_inverse[...])

    landed(gram.at[pl.ds(0, 31 * 8)], gc_recv)
    inner = lower_half(
        base[...]
        - lax.dot_general(
            chain[...], gram[...], (((1,), (1,)), ((), ())),
            precision=HIGHEST, preferred_element_type=F32,
        )
    )
    left = dot(inverse_t[...], inner)
    diag_grad[...] = lower_half(dot(left, diag_inverse[...]))

    for condition, copy in sent:
        if condition is None:
            copy.wait_send()
        else:
            pl.when(condition)(copy.wait_send)


def on_device(trail_adjoint, panel, panel_adjoint, diag_factor, diag_inverse, diag_adjoint):
    vmem = pl.BlockSpec(memory_space=pltpu.VMEM)
    dma = pltpu.SemaphoreType.DMA
    return pl.pallas_call(
        kernel,
        out_shape=(
            jax.ShapeDtypeStruct((ROWS, WIDE), F32),
            jax.ShapeDtypeStruct((WIDE, WIDE), F32),
        ),
        in_specs=[pl.BlockSpec(memory_space=pl.ANY)] + [vmem] * 5,
        out_specs=(vmem, vmem),
        scratch_shapes=[
            pltpu.VMEM((4, CHUNK, CHUNK), F32),
            pltpu.VMEM((4, CHUNK, CHUNK), BF16),
            pltpu.VMEM((4, CHUNK, CHUNK), BF16),
            pltpu.VMEM((4, 8, ROWS, WIDE), F32),
            pltpu.VMEM((4, FIRST, WIDE), F32),
            pltpu.VMEM((CHUNK, WIDE), BF16),
            pltpu.VMEM((CHUNK, WIDE), BF16),
            pltpu.VMEM((CHUNK, WIDE), F32),
            pltpu.VMEM((8, ROWS, WIDE), F32),
            pltpu.VMEM((WIDE, CHUNK), BF16),
            pltpu.VMEM((WIDE, CHUNK), BF16),
            pltpu.VMEM((WIDE, WIDE), F32),
            pltpu.VMEM((WIDE, WIDE), F32),
            pltpu.VMEM((WIDE, WIDE), F32),
            pltpu.VMEM((WIDE, WIDE), F32),
            pltpu.VMEM((WIDE, WIDE), F32),
            pltpu.VMEM((32, 8, WIDE), F32),
            pltpu.VMEM((8, WIDE), F32),
            pltpu.VMEM((8, 8, WIDE), F32),
            pltpu.VMEM((WIDE, WIDE), F32),
            pltpu.VMEM((4, ROWS, WIDE), F32),
            pltpu.VMEM((4, ROWS, WIDE), F32),
            pltpu.VMEM((3, ROWS, WIDE), F32),
            dma((4,)),
            dma((3,)), dma((4,)), dma((4,)), dma, dma((2, 4, 4)), dma((2, 4, 4)),
            dma, dma, dma((2, 4)), dma((2, 4)), dma((2, 5, 3)), dma((4,)),
            dma((7,)), dma, dma((4,)), dma, dma((3,)), dma,
            dma((31,)), dma, dma((7,)), dma, dma((31,)), dma,
        ],
        compiler_params=pltpu.CompilerParams(
            collective_id=0, has_side_effects=True, vmem_limit_bytes=56 * 1024 * 1024
        ),
    )(trail_adjoint, panel, panel_adjoint, diag_factor, diag_inverse, diag_adjoint)


def solution(mesh):
    in_specs = (P("row", "col"), P(("row", "col"), None), P(("row", "col"), None), P(), P(), P())
    out_specs = (P(("row", "col"), None), P())
    return jax.shard_map(
        on_device, mesh=mesh, in_specs=in_specs, out_specs=out_specs, check_vma=False
    )
```

time: 523 us -> 72.6 us (0.14)
  waiting for transfers between devices: 468 us -> 0 us
  Pallas kernels: 0 us -> 68.6 us
  blocking collectives: 17.9 us -> 0 us
  matrix products: 16.3 us -> 0 us
  between operations: 13.9 us -> 0.64 us
    psum x1 -> x0, waiting for transfers between devices: 255 us -> none  [on_device(): gram = lax.psum(local_gram, ('row', 'col'))]
    all_gather x1 -> x0, waiting for transfers between devices: 184 us -> none  [on_device(): full_panel = lax.all_gather(row_block, 'row', axis=0, tiled=True)]
    pallas_call x0 -> x1, Pallas kernels: none -> 68.6 us  [on_device(): pl.pallas_call(kernel, out_shape=(jax.ShapeDtypeStruct((ROWS, WIDE), F32)...]
    reduce_scatter x1 -> x0, waiting for transfers between devices: 29.1 us -> none  [on_device(): lax.psum_scatter(jnp.dot(trail_adjoint, column_panel, precision=highest,...]
    all_gather x1 -> x0, blocking collectives: 17.9 us -> none  [on_device(): row_block = lax.all_gather(panel, 'col', axis=0, tiled=True)]
    dot_general x6 -> x0, matrix products: 16.3 us -> none  [the longest x1 11.5 us: on_device(): jnp.dot(trail_adjoint, column_panel, precision=highest, preferred_element...]
  transfers between devices with their start and end apart: 3 -> 0, of which waited for: 3 -> 0; matrix products, arithmetic and copies ran while one was open for 0% -> 0% of each run, Pallas kernels for 0% -> 0%
where the time goes in v2:
time: 72.6 us; the launch traced here: 72.5 us
  Pallas kernels  68.6 us (94%)
  local copies, waits for them, and re-layouts  3.21 us (4%)
    pallas_call x1, Pallas kernels, on_device(): pl.pallas_call(kernel, out_shape=(jax.ShapeDtypeStruct((ROWS, WIDE), F32)...  68.6 us
    unnamed x2, local copies, waits for them, and re-layouts  3.21 us

profile of v2, /device:TPU:1, one launch (start us, length us, event | category | flops | bytes accessed | tf_op | source)
XLA Modules:
  0.0 72.5 jit_solution(4412688499853647785)
XLA Ops:
  0.6 68.6 %shard_map.77 = (f32[96,256]{1,0:T(8,128)}, f32[256,256]{1,0:T(8,128)}) custom-call(f32[768,3072]{1,0:T(8,128)} %trail.1, f32[96,256]{1,0:T(8,128)} %panel.1, f32[96,256]{1,0:T(8,128)} %panel_adjoint.1, f32[256,256]{1,0:T(8,128)} %diag_factor.1, f32[256,256]{1,0:T(8,128)} %diag_inverse.1, f32[256,256]{1,0:T(8,128)} %diag_adjoint.1), custom_call_target="tpu_custom_call" | custom-call | tf_op jit(solution)/shard_map/pallas_call | solution.py:353
  69.3 1.5 %copy.10 = f32[96,256]{1,0:T(8,128)} copy(f32[96,256]{1,0:T(8,128)} %get-tuple-element.4) | data formatting | bytes 196608
  70.8 1.7 %copy.11 = f32[256,256]{1,0:T(8,128)} copy(f32[256,256]{1,0:T(8,128)} %get-tuple-element.5) | data formatting | bytes 524288

commit v3 on v2

--- a/solution.py
+++ b/solution.py
@@ -14,7 +14,8 @@
 ROWS = 96
 WIDE = 256
 CHUNK = 768
-FIRST = 40
+CUT = 24
+FIRST = 48
 SECOND = ROWS - FIRST
 
 
@@ -29,16 +30,17 @@
 
 
 def kernel(
-    trail, panel, panel_adjoint, diag_factor, diag_inverse, diag_adjoint,
+    trail, panel_in, panel_adjoint_in, diag_factor_in, diag_inverse_in, diag_adjoint_in,
     panel_grad, diag_grad,
-    raw, high, low, gathered, stage, p_high, p_low, image,
+    panel, panel_adjoint, diag_factor, diag_inverse, diag_adjoint,
+    raw, high, low, gathered, ring, lines, stage, p_high, p_low, image,
     row_panel, turned_high, turned_low, early, chain, base, inverse_t,
     gram_local, gram_parts, slab, slab_parts, gram,
     core_parts, x_source, x_parts,
-    trail_sem,
+    z_known, plane_known, input_sem, trail_sem,
     s1y_send, s1y_recv, s1x_send, s1u_recv, s1z_send, s1z_recv,
-    s2r_send, s2r_recv, s2z_send, s2z_recv, s2y_send, s2y_recv,
-    rp_send, rp_recv, rc_send, rc_recv, rx_send, rx_recv,
+    s2z_send, s2z_recv, s2y_send, s2y_recv, s2x_send, s2x_recv,
+    rp_send, rp_recv, rf_send, rf_recv, rc_send, rc_recv, rx_send, rx_recv,
     ga_send, ga_recv, gb_send, gb_recv, gc_send, gc_recv,
 ):
     r = lax.axis_index("row")
@@ -46,15 +48,6 @@
     y, z = r // NZ, r % NZ
     x, c = q // 2, q % 2
     half = z // 4
-
-    loads = [
-        pltpu.make_async_copy(
-            trail.at[:, pl.ds(j * CHUNK, CHUNK)], raw.at[j], trail_sem.at[j]
-        )
-        for j in range(4)
-    ]
-    for load in loads:
-        load.start()
 
     def col_peer(dx, dc):
         return ((x + dx) % NX) * 2 + (c + dc) % 2
@@ -77,10 +70,36 @@
     def greet(row, col):
         pl.semaphore_signal(barrier, inc=1, device_id=(row, col), device_id_type=MESH)
 
-    for peer in plane:
-        greet(*plane_peer(*peer))
-    for dz in depth:
-        greet(y * NZ + (z + dz) % NZ, q)
+    towards = (y * NZ + (z + 1) % NZ, y * NZ + (z + 7) % NZ)
+    across = [((y + dy) % NY) * NZ + z for dy in (2, 1, 3)]
+    for row in across:
+        greet(row, q)
+    for dx, dc in row_peers:
+        greet(r, col_peer(dx, dc))
+    for row in towards:
+        greet(row, q)
+
+    def tell(sem, rows):
+        for row in rows:
+            pl.semaphore_signal(sem, inc=1, device_id=(row, q), device_id_type=MESH)
+
+    small = [
+        pltpu.make_async_copy(src, dst, input_sem.at[n])
+        for n, (src, dst) in enumerate((
+            (panel_in, panel), (diag_factor_in, diag_factor), (diag_inverse_in, diag_inverse),
+            (diag_adjoint_in, diag_adjoint), (panel_adjoint_in, panel_adjoint),
+        ))
+    ]
+    for load in small:
+        load.start()
+    loads = [
+        pltpu.make_async_copy(
+            trail.at[:, pl.ds(j * CHUNK, CHUNK)], raw.at[j], trail_sem.at[j]
+        )
+        for j in range(4)
+    ]
+    for load in loads:
+        load.start()
 
     sent = []
 
@@ -108,21 +127,22 @@
 
         sent.append((jnp.logical_not(own), copy))
 
+    events_of = ((0, 0), (0, 1), (1, 1), (0, 2), (1, 2), (0, 3), (1, 3), (0, 4))
     top, bottom = pl.ds(0, FIRST), pl.ds(FIRST, SECOND)
-    towards = (y * NZ + (z + 1) % NZ, y * NZ + (z + 7) % NZ)
 
     def origin(way, s):
         return (z - s + 8) % NZ if way == 0 else (z + s) % NZ
 
     def top_copy(o, way, s, part):
-        ref = gathered.at[o % 4, pl.ds(2 * part, 2), top]
+        ref = gathered.at[o % 4, pl.ds(2 * ((x + part) % NX), 2), top]
         return remote(
             ref, ref, s1z_send.at[way, s - 1, part], s1z_recv.at[way, s - 1, part], towards[way], q
         )
 
     def bottom_copy(o, way, s):
-        items = pl.ds(2 * y, 2) if s < 4 else pl.ds(2 * y + way, 1)
-        ref = gathered.at[o % 4, items, bottom]
+        ref = ring.at[o]
+        if s == 4:
+            ref = ring.at[o, pl.ds(0, CUT)] if way == 0 else ring.at[o, pl.ds(CUT, SECOND - CUT)]
         return remote(ref, ref, s2z_send.at[way, s - 1], s2z_recv.at[way, s - 1], towards[way], q)
 
     def carried(way, s, part):
@@ -149,38 +169,39 @@
 
     def bottom_start(s):
         for way in range(2):
-            o = origin(way, s - 1)
-            copy = bottom_copy(o, way, s)
-            pl.when(o // 4 == c)(copy.start)
-            sent.append((o // 4 == c, copy))
+            go(bottom_copy(origin(way, s - 1), way, s))
 
     def bottom_wait(s):
         for way in range(2):
-            o = origin(way, s)
-            pl.when(o // 4 == c)(bottom_copy(o, way, s).wait_recv)
-
-    def bottom_step(s):
-        bottom_wait(s)
-        bottom_start(s + 1)
-        s2y(0, s)
-        s2y(1, s)
+            bottom_copy(origin(way, s), way, s).wait_recv()
 
     def s1x(a, src, n):
         dst = gathered.at[z % 4, q, top]
-        copy = remote(src, dst, s1x_send.at[n], s1u_recv, r, 2 * a + half)
-        one_or_local(copy, (x == a) & (half == c), src, dst, s1u_recv)
-
-    def s2y(way, s):
-        o = origin(way, s)
-        mine = o // 4 == c
-        ref = gathered.at[o % 4, pl.ds(2 * y, 2), bottom]
-        for n, dy in enumerate((2, 1, 3)):
-            copy = remote(
-                ref, ref, s2y_send.at[way, s, n], s2y_recv.at[o % 4],
-                ((y + dy) % NY) * NZ + z, q,
-            )
-            pl.when(mine)(copy.start)
-            sent.append((mine, copy))
+        copy = remote(src, dst, s1x_send.at[n], s1u_recv.at[x], r, 2 * a + half)
+        one_or_local(copy, (x == a) & (half == c), src, dst, s1u_recv.at[x])
+
+    def s2x(e, o, a, src, n):
+        dst = gathered.at[o % 4, q, bottom]
+        copy = remote(src, dst, s2x_send.at[e, n], s2x_recv.at[o % 4], r, 2 * a + o // 4)
+        one_or_local(copy, (x == a) & (o // 4 == c), src, dst, s2x_recv.at[o % 4])
+
+    def s2_out(*events):
+        for e in events:
+            o = origin(*events_of[e])
+            for n, dy in enumerate((2, 1, 3)):
+                go(remote(
+                    ring.at[o], lines.at[y, o], s2y_send.at[e, n], s2y_recv.at[e, n],
+                    ((y + dy) % NY) * NZ + z, q,
+                ))
+            s2x(e, o, y, ring.at[o], 3)
+
+    def s2_across(*events):
+        for e in events:
+            o = origin(*events_of[e])
+            for n, dy in ((1, 1), (2, 3), (0, 2)):
+                a = (y - dy + NY) % NY
+                landed(lines.at[a, o], s2y_recv.at[e, n])
+                s2x(e, o, a, lines.at[a, o], n)
 
     def split_trail(j):
         loads[j].wait()
@@ -193,96 +214,115 @@
             high[j, rows, :] = head
             low[j, rows, :] = (value - head.astype(F32)).astype(BF16)
 
-    def multiply(o):
+    def multiply(way, s):
+        o = origin(way, s)
+
         @pl.when(o // 4 == c)
         def _():
             j = o % 4
-            landed(gathered.at[j, pl.ds(0, 6), bottom], s2y_recv.at[j])
+            landed(gathered.at[j, :, bottom], s2x_recv.at[j])
             block = gathered[j].reshape(CHUNK, WIDE)
             head = block.astype(BF16)
             p_high[...] = head
             p_low[...] = (block - head.astype(F32)).astype(BF16)
 
-            @pl.loop(0, CHUNK, step=256)
-            def _(i):
-                rows = pl.ds(pl.multiple_of(i, 256), 256)
-                a, b = high[j, rows, :], low[j, rows, :]
-                image[rows, :] += (
-                    jnp.dot(a, p_high[...], preferred_element_type=F32)
-                    + jnp.dot(a, p_low[...], preferred_element_type=F32)
-                    + jnp.dot(b, p_high[...], preferred_element_type=F32)
-                )
+            image[...] += (
+                jnp.dot(high[j], p_high[...], preferred_element_type=F32)
+                + jnp.dot(high[j], p_low[...], preferred_element_type=F32)
+                + jnp.dot(low[j], p_high[...], preferred_element_type=F32)
+            )
 
     image[...] = jnp.zeros_like(image)
+    for load in small:
+        load.wait()
     row_panel[q] = panel[...]
-    inverse_t[...] = diag_inverse[...].T
-    factor_t = diag_factor[...].T
-    chain[...] = dot(factor_t, inverse_t[...])
-    base[...] = dot(factor_t, diag_adjoint[...])
-    early[...] = dot(panel[...].T, panel_adjoint[...])
-    for j in range(4):
-        split_trail(j)
-    pl.semaphore_wait(barrier, len(plane) + len(depth))
+    ring[z] = panel[FIRST:, :]
+    split_trail(0)
+    split_trail(1)
+    pl.semaphore_wait(barrier, 3 + 7 + 2)
+    tell(z_known.at[0], towards)
+    tell(plane_known, across)
 
     for n, dy in enumerate((2, 1, 3)):
         go(remote(
             panel.at[top], stage.at[3 - n], s1y_send.at[n], s1y_recv.at[3 - n],
             ((y + dy) % NY) * NZ + z, q,
         ))
-    s2r_dst = gathered.at[z % 4, q, bottom]
-    s2r = remote(panel.at[bottom], s2r_dst, s2r_send, s2r_recv, x * NZ + z, 2 * y + half)
-    one_or_local(s2r, (x == y) & (half == c), panel.at[bottom], s2r_dst, s2r_recv)
+    bottom_start(1)
+    for n, (dx, dc) in enumerate(((2, 0), (1, 0), (3, 0), (0, 1))):
+        go(remote(panel, row_panel.at[q], rp_send.at[n], rp_recv.at[n], r, col_peer(dx, dc)))
+    s2_out(0)
     s1x(y, panel.at[top], 0)
+    split_trail(2)
     for n, dy in ((1, 1), (2, 3), (0, 2)):
         landed(stage.at[3 - n], s1y_recv.at[3 - n])
         s1x((y - dy + NY) % NY, stage.at[3 - n], 3 - n)
 
-    @pl.when(half == c)
-    def _():
-        landed(gathered.at[z % 4, pl.ds(0, 2), bottom], s2r_recv)
-
-    bottom_start(1)
-    s2y(0, 0)
-    for n, (dx, dc) in enumerate(row_peers):
-        go(remote(panel, row_panel.at[q], rp_send.at[n], rp_recv, r, col_peer(dx, dc)))
-
-    @pl.when(half == c)
-    def _():
-        landed(gathered.at[z % 4, :, top], s1u_recv)
-
-    for part in range(4):
+    def top_root(part):
+        @pl.when(half == c)
+        def _():
+            landed(gathered.at[z % 4, pl.ds(0, 2), top], s1u_recv.at[(x + part) % NX])
+
         top_start(1, part)
-    bottom_step(1)
+
+    bottom_wait(1)
+    bottom_start(2)
+    s2_out(1, 2)
+    s2_across(0)
+    top_root(0)
+    bottom_wait(2)
+    bottom_start(3)
+    pl.semaphore_wait(z_known.at[0], 2)
+    tell(z_known.at[1], towards)
+    s2_out(3, 4)
+    top_root(1)
+    top_root(3)
+    split_trail(3)
+    s2_across(1, 2)
+    top_root(2)
+    for n, dx in ((1, 1), (2, 3), (0, 2)):
+        ref = row_panel.at[2 * ((x - dx + NX) % NX) + c]
+        landed(ref, rp_recv.at[n])
+        go(remote(ref, ref, rf_send.at[n], rf_recv, r, col_peer(0, 1)))
+    landed(row_panel.at[0], rp_recv.at[3])
+    bottom_wait(3)
+    bottom_start(4)
+    pl.semaphore_wait(z_known.at[1], 2)
+    tell(z_known.at[2], towards)
+    s2_out(5, 6)
     top_step(1, 0, 1)
-    bottom_step(2)
-    top_step(1, 2, 3)
-    multiply(z)
-    top_step(2, 0, 1)
-    bottom_step(3)
-    top_step(2, 2, 3)
-    multiply(origin(0, 1))
-    multiply(origin(1, 1))
-    top_wait(3, 0)
-    top_start(4, 0)
-    top_wait(3, 1)
-    top_start(4, 1)
-    top_wait(3, 2)
-    top_start(4, 2)
-    top_wait(3, 3)
-    top_start(4, 3)
-    bottom_wait(4)
-    s2y(0, 4)
-    landed(row_panel.at[pl.ds(0, 7)], rp_recv)
+    s2_across(3, 4)
+    top_step(1, 3, 2)
+    landed(row_panel.at[pl.ds(0, 3)], rf_recv)
     turned = row_panel[...].reshape(CHUNK, WIDE).T
     turned_head = turned.astype(BF16)
     turned_high[...] = turned_head
     turned_low[...] = (turned - turned_head.astype(F32)).astype(BF16)
-    for s in (2, 3):
-        multiply(origin(0, s))
-        multiply(origin(1, s))
+    inverse_t[...] = diag_inverse[...].T
+    factor_t = diag_factor[...].T
+    chain[...] = dot(factor_t, inverse_t[...])
+    bottom_wait(4)
+    s2_out(7)
+    pl.semaphore_wait(z_known.at[2], 2)
+    pl.semaphore_wait(plane_known, 3)
+    top_step(2, 0, 1)
+    s2_across(5, 6)
+    base[...] = dot(diag_factor[...].T, diag_adjoint[...])
+    early[...] = dot(panel[...].T, panel_adjoint[...])
+    top_step(2, 3, 2)
+    s2_across(7)
+    multiply(0, 0)
+    multiply(0, 1)
+    multiply(1, 1)
+    top_step(3, 0, 1)
+    multiply(0, 2)
+    multiply(1, 2)
+    top_step(3, 3, 2)
+    multiply(0, 3)
+    multiply(1, 3)
     for part in range(4):
         top_wait(4, part)
-    multiply(origin(0, 4))
+    multiply(0, 4)
 
     for n in range(4):
         block = pl.ds(pl.multiple_of((2 * n + 1 - c) * ROWS, ROWS), ROWS)
@@ -356,13 +396,20 @@
             jax.ShapeDtypeStruct((ROWS, WIDE), F32),
             jax.ShapeDtypeStruct((WIDE, WIDE), F32),
         ),
-        in_specs=[pl.BlockSpec(memory_space=pl.ANY)] + [vmem] * 5,
+        in_specs=[pl.BlockSpec(memory_space=pltpu.HBM)] * 6,
         out_specs=(vmem, vmem),
         scratch_shapes=[
+            pltpu.VMEM((ROWS, WIDE), F32),
+            pltpu.VMEM((ROWS, WIDE), F32),
+            pltpu.VMEM((WIDE, WIDE), F32),
+            pltpu.VMEM((WIDE, WIDE), F32),
+            pltpu.VMEM((WIDE, WIDE), F32),
             pltpu.VMEM((4, CHUNK, CHUNK), F32),
             pltpu.VMEM((4, CHUNK, CHUNK), BF16),
             pltpu.VMEM((4, CHUNK, CHUNK), BF16),
             pltpu.VMEM((4, 8, ROWS, WIDE), F32),
+            pltpu.VMEM((8, SECOND, WIDE), F32),
+            pltpu.VMEM((4, 8, SECOND, WIDE), F32),
             pltpu.VMEM((4, FIRST, WIDE), F32),
             pltpu.VMEM((CHUNK, WIDE), BF16),
             pltpu.VMEM((CHUNK, WIDE), BF16),
@@ -382,10 +429,11 @@
             pltpu.VMEM((4, ROWS, WIDE), F32),
             pltpu.VMEM((4, ROWS, WIDE), F32),
             pltpu.VMEM((3, ROWS, WIDE), F32),
-            dma((4,)),
-            dma((3,)), dma((4,)), dma((4,)), dma, dma((2, 4, 4)), dma((2, 4, 4)),
-            dma, dma, dma((2, 4)), dma((2, 4)), dma((2, 5, 3)), dma((4,)),
-            dma((7,)), dma, dma((4,)), dma, dma((3,)), dma,
+            pltpu.SemaphoreType.REGULAR((3,)), pltpu.SemaphoreType.REGULAR,
+            dma((5,)), dma((4,)),
+            dma((3,)), dma((4,)), dma((4,)), dma((4,)), dma((2, 4, 4)), dma((2, 4, 4)),
+            dma((2, 4)), dma((2, 4)), dma((8, 3)), dma((8, 3)), dma((8, 4)), dma((4,)),
+            dma((4,)), dma((4,)), dma((3,)), dma, dma((4,)), dma, dma((3,)), dma,
             dma((31,)), dma, dma((7,)), dma, dma((31,)), dma,
         ],
         compiler_params=pltpu.CompilerParams(

time: 72.6 us -> 69.7 us (0.960)
  Pallas kernels: 68.6 us -> 65.7 us
    pallas_call x1, Pallas kernels: 68.6 us -> 65.7 us  [on_device(): pl.pallas_call(kernel, out_shape=(jax.ShapeDtypeStruct((ROWS, WIDE), F32)...]
where the time goes in v3:
time: 69.7 us; the launch traced here: 69.6 us
  Pallas kernels  65.7 us (94%)
  local copies, waits for them, and re-layouts  3.21 us (5%)
    pallas_call x1, Pallas kernels, on_device(): pl.pallas_call(kernel, out_shape=(jax.ShapeDtypeStruct((ROWS, WIDE), F32)...  65.7 us
    unnamed x2, local copies, waits for them, and re-layouts  3.21 us

profile of v3, /device:TPU:1, one launch (start us, length us, event | category | flops | bytes accessed | tf_op | source)
XLA Modules:
  0.0 69.6 jit_solution(8342150688198336545)
XLA Ops:
  0.6 65.7 %shard_map.77 = (f32[96,256]{1,0:T(8,128)}, f32[256,256]{1,0:T(8,128)}) custom-call(f32[768,3072]{1,0:T(8,128)} %trail.1, f32[96,256]{1,0:T(8,128)} %panel_in.1, f32[96,256]{1,0:T(8,128)} %panel_adjoint_in.1, f32[256,256]{1,0:T(8,128)} %diag_factor_in.1, f32[256,256]{1,0:T(8,128)} %diag_inverse_in.1, f32[256,256]{1,0:T(8,128)} %diag_adjoint_in.1), custom_call_target="tpu_custom_call" | custom-call | tf_op jit(solution)/shard_map/pallas_call | solution.py:393
  66.4 1.5 %copy.10 = f32[96,256]{1,0:T(8,128)} copy(f32[96,256]{1,0:T(8,128)} %get-tuple-element.4) | data formatting | bytes 196608
  67.9 1.7 %copy.11 = f32[256,256]{1,0:T(8,128)} copy(f32[256,256]{1,0:T(8,128)} %get-tuple-element.5) | data formatting | bytes 524288

commit v4 on v3

--- a/solution.py
+++ b/solution.py
@@ -387,10 +387,23 @@
             pl.when(condition)(copy.wait_send)
 
 
+def hand_over(grad, diag, grad_out, diag_out, grad_held, diag_held, sem):
+    ways = ((diag, diag_held, diag_out), (grad, grad_held, grad_out))
+    into = [pltpu.make_async_copy(src, held, sem.at[0, n]) for n, (src, held, _) in enumerate(ways)]
+    out = [pltpu.make_async_copy(held, dst, sem.at[1, n]) for n, (_, held, dst) in enumerate(ways)]
+    for copy in into:
+        copy.start()
+    for landing, leaving in zip(into, out):
+        landing.wait()
+        leaving.start()
+    for copy in out:
+        copy.wait()
+
+
 def on_device(trail_adjoint, panel, panel_adjoint, diag_factor, diag_inverse, diag_adjoint):
     vmem = pl.BlockSpec(memory_space=pltpu.VMEM)
     dma = pltpu.SemaphoreType.DMA
-    return pl.pallas_call(
+    results = pl.pallas_call(
         kernel,
         out_shape=(
             jax.ShapeDtypeStruct((ROWS, WIDE), F32),
@@ -440,6 +453,18 @@
             collective_id=0, has_side_effects=True, vmem_limit_bytes=56 * 1024 * 1024
         ),
     )(trail_adjoint, panel, panel_adjoint, diag_factor, diag_inverse, diag_adjoint)
+    anywhere = pl.BlockSpec(memory_space=pl.ANY)
+    return pl.pallas_call(
+        hand_over,
+        out_shape=(
+            jax.ShapeDtypeStruct((ROWS, WIDE), F32),
+            jax.ShapeDtypeStruct((WIDE, WIDE), F32),
+        ),
+        in_specs=[anywhere] * 2,
+        out_specs=(anywhere,) * 2,
+        scratch_shapes=[pltpu.VMEM((ROWS, WIDE), F32), pltpu.VMEM((WIDE, WIDE), F32), dma((2, 2))],
+        compiler_params=pltpu.CompilerParams(vmem_limit_bytes=56 * 1024 * 1024),
+    )(*results)
 
 
 def solution(mesh):

time: 69.7 us -> 68.3 us (0.980)
  local copies, waits for them, and re-layouts: 3.21 us -> 0 us
  Pallas kernels: 65.7 us -> 67.4 us
    unnamed x2 -> x0, local copies, waits for them, and re-layouts: 3.21 us -> none
    pallas_call x0 -> x1, Pallas kernels: none -> 1.71 us  [on_device(): pl.pallas_call(hand_over, out_shape=(jax.ShapeDtypeStruct((ROWS, WIDE), F...]
where the time goes in v4:
time: 68.3 us; the launch traced here: 68.2 us
  Pallas kernels  67.4 us (99%)
  between operations  0.8 us (1%)
    pallas_call x1, Pallas kernels, on_device(): pl.pallas_call(kernel, out_shape=(jax.ShapeDtypeStruct((ROWS, WIDE), F32)...  65.7 us
    pallas_call x1, Pallas kernels, on_device(): pl.pallas_call(hand_over, out_shape=(jax.ShapeDtypeStruct((ROWS, WIDE), F...  1.71 us

profile of v4, /device:TPU:1, one launch (start us, length us, event | category | flops | bytes accessed | tf_op | source)
XLA Modules:
  0.0 68.2 jit_solution(4535731704798530621)
XLA Ops:
  0.6 65.7 %shard_map.77 = (f32[96,256]{1,0:T(8,128)}, f32[256,256]{1,0:T(8,128)}) custom-call(f32[768,3072]{1,0:T(8,128)} %trail.1, f32[96,256]{1,0:T(8,128)} %panel_in.1, f32[96,256]{1,0:T(8,128)} %panel_adjoint_in.1, f32[256,256]{1,0:T(8,128)} %diag_factor_in.1, f32[256,256]{1,0:T(8,128)} %diag_inverse_in.1, f32[256,256]{1,0:T(8,128)} %diag_adjoint_in.1), custom_call_target="tpu_custom_call" | custom-call | tf_op jit(solution)/shard_map/pallas_call | solution.py:406
  66.4 1.7 %shard_map.78 = (f32[96,256]{1,0:T(8,128)}, f32[256,256]{1,0:T(8,128)}) custom-call(f32[96,256]{1,0:T(8,128)} %get-tuple-element.4.grad, f32[256,256]{1,0:T(8,128)} %get-tuple-element.5.diag), custom_call_target="tpu_custom_call" | custom-call | tf_op jit(solution)/shard_map/pallas_call | solution.py:457
